TPU v7x, 32 devices: a whole 2x2x4 slice. The times are simulated.
32 devices in a mesh: vox: 4 (over x, core), mem: 8 (over z, y).
Axes of the slice: x: 2, y: 2, z: 4, core: 2. Of those that a mesh axis runs over, the one named last changes fastest.
Arguments:
- ensemble: bfloat16 [256, 65536], P('mem', 'vox'), may hold values from -6 to 6
- partials: float32 [4, 256, 16384], P('vox', 'mem'), may hold values from -6 to 6
- perturb: float32 [256, 16384], P('mem', 'vox'), may hold values from -6 to 6
- observed: float32 [16384], P('vox'), may hold values from -6 to 6
- variance: float32 [16384], P('vox'), may hold values from 0.5 to 2
- obs_lists: int32 [512, 16], P(('vox', 'mem')), may hold values from 0 to 31, all different within a row
- taper_index: int32 [512, 16], P(('vox', 'mem')), may hold values from 0 to 15
- taper_table: float32 [16], replicated, may hold values from 0.1 to 1
Outputs:
- updated: bfloat16 [256, 65536], P('mem', 'vox')
All inputs are finite; a program needn't handle non-finite values.
Results may differ from a plain program's by a relative error of at most 0.017.
Values may be sent and summed in bfloat16 or wider, within the bound.
No kernel may reach another device: no remote copies, remote signals or barrier semaphores. Data moves between devices by JAX's collectives and lax.ppermute only.
A program may use at most 128 MiB of HBM per device.

v0:
```python
import jax
import jax.numpy as jnp
from jax import lax
from jax.sharding import PartitionSpec as P

OB = 128


def center(values):
    as_float = values.astype(jnp.float32)
    return (as_float - jnp.mean(as_float, axis=0, keepdims=True)).astype(jnp.bfloat16)


def block_moments(obs_anom, weights):
    return jnp.einsum("kbi,lbi->bkl", obs_anom, weights, preferred_element_type=jnp.float32)


def from_moments(moments, coeff, state_anom):
    high = lax.Precision.HIGHEST
    combined = jnp.einsum("bo,okl->bkl", coeff, moments, precision=high).astype(jnp.bfloat16)
    return jnp.einsum("kbc,bkl->lbc", state_anom, combined, preferred_element_type=jnp.float32)


def local(ensemble, partials, perturb, observed, variance, obs_lists, taper_index, taper_table):
    summed = lax.psum_scatter(
        partials[0].astype(jnp.bfloat16), "vox", scatter_dimension=1, tiled=True
    )
    weights = (
        (observed[None, :] + perturb - summed.astype(jnp.float32)) / variance[None, :]
    ).astype(jnp.bfloat16)
    members = lax.all_to_all(ensemble, "mem", split_axis=1, concat_axis=0, tiled=True)
    count = members.shape[0]
    blocks = obs_lists.shape[0]
    cells = members.shape[1] // blocks
    groups = weights.shape[1] // OB
    state_anom = center(members).reshape(count, blocks, cells)
    table_hits = (
        taper_index[:, :, None] == jnp.arange(taper_table.shape[0], dtype=jnp.int32)[None, None, :]
    ).astype(jnp.float32)
    tapers = jnp.sum(table_hits * taper_table[None, None, :], axis=2)
    picks = (obs_lists[:, :, None] == jnp.arange(groups, dtype=jnp.int32)[None, None, :]).astype(
        jnp.float32
    )
    coeff = jnp.sum(tapers[:, :, None] * picks, axis=1)
    pred_own, wts_own = (
        lax.all_to_all(summed, "mem", split_axis=1, concat_axis=0, tiled=True),
        lax.all_to_all(weights, "mem", split_axis=1, concat_axis=0, tiled=True),
    )
    own_anom = center(pred_own).reshape(count, -1, OB)
    own_moments = block_moments(own_anom, wts_own.reshape(count, -1, OB))
    moments = lax.all_gather(own_moments.astype(jnp.bfloat16), "mem", axis=0, tiled=True).astype(
        own_moments.dtype
    )
    increment = from_moments(moments, coeff, state_anom).reshape(count, blocks * cells)
    updated = (members.astype(jnp.float32) + increment * (1.0 / (count - 1))).astype(jnp.bfloat16)
    return lax.all_to_all(updated, "mem", split_axis=0, concat_axis=1, tiled=True)


def solution(mesh):
    return jax.shard_map(
        local,
        mesh=mesh,
        in_specs=(
            P("mem", "vox"),
            P("vox", "mem", None),
            P("mem", "vox"),
            P("vox"),
            P("vox"),
            P(("vox", "mem"), None),
            P(("vox", "mem"), None),
            P(),
        ),
        out_specs=P("mem", "vox"),
        check_vma=False,
    )
```

profile of v0, /device:TPU:0, one launch (start us, length us, event | category | flops | bytes accessed | tf_op | source)
XLA Modules:
  0.0 203.3 jit_solution(8342497593390177636)
XLA Ops:
  6.5 2.7 %convert_bitcast_fusion = bf16[32,16384]{1,0:T(8,128)(2,1)} fusion(f32[1,32,16384]{2,1,0:T(8,128)} %param.9), kind=kLoop, calls=%fused_computation.13 | loop fusion | flops 524288 | bytes 3145728 | tf_op jit(solution)/shard_map/convert_element_type | solution.py:26
  9.3 28.1 %reduce-scatter.2.cloned.1.call-done = bf16[32,4096]{1,0:T(8,128)(2,1)} async-done(((bf16[32,16384]{1,0:T(8,128)(2,1)}), bf16[32,4096]{1,0:T(8,128)(2,1)}) %reduce-scatter.2.cloned.1.call-update) | async-done | bytes 262160 | tf_op jit(solution)/shard_map/reduce_scatter | solution.py:25
  37.4 1.7 copy.67
  39.1 5.5 %all-to-all-start.1 = ((bf16[32,8,512]{2,0,1:T(8,128)(2,1)}), bf16[32,8,512]{2,0,1:T(8,128)(2,1)S(1)}, u32[]{:S(2)}, u32[]{:S(2)}) async-start(bf16[32,8,512]{2,0,1:T(8,128)(2,1)} %bitcast.38), calls=%async_computation.2 | async-start | bytes 524288 | tf_op jit(solution)/shard_map/all_to_all | solution.py:46
  44.6 1.0 divide_convert_fusion
  45.7 0.7 copy.66
  46.4 7.0 %all-to-all-done.1 = bf16[32,8,512]{2,0,1:T(8,128)(2,1)S(1)} async-done(((bf16[32,8,512]{2,0,1:T(8,128)(2,1)}), bf16[32,8,512]{2,0,1:T(8,128)(2,1)S(1)}, u32[]{:S(2)}, u32[]{:S(2)}) %all-to-all-start.1) | async-done | bytes 262176 | tf_op jit(solution)/shard_map/all_to_all | solution.py:46
  53.3 3.6 %all-to-all-start.2 = ((bf16[32,8,512]{2,0,1:T(8,128)(2,1)}), bf16[32,8,512]{2,0,1:T(8,128)(2,1)S(1)}, u32[]{:S(2)}, u32[]{:S(2)}) async-start(bf16[32,8,512]{2,0,1:T(8,128)(2,1)} %bitcast.37), calls=%async_computation.3 | async-start | bytes 524288 | tf_op jit(solution)/shard_map/all_to_all | solution.py:47
  57.3 8.2 %all-to-all-done.2 = bf16[32,8,512]{2,0,1:T(8,128)(2,1)S(1)} async-done(((bf16[32,8,512]{2,0,1:T(8,128)(2,1)}), bf16[32,8,512]{2,0,1:T(8,128)(2,1)S(1)}, u32[]{:S(2)}, u32[]{:S(2)}) %all-to-all-start.2) | async-done | bytes 262176 | tf_op jit(solution)/shard_map/all_to_all | solution.py:47
  65.7 1.1 convolution_convert_fusion
  66.9 1.0 copy.65
  67.9 3.6 %all-to-all-start = ((bf16[32,8,2048]{2,0,1:T(8,128)(2,1)}), bf16[32,8,2048]{2,0,1:T(8,128)(2,1)S(1)}, u32[]{:S(2)}, u32[]{:S(2)}) async-start(bf16[32,8,2048]{2,0,1:T(8,128)(2,1)} %bitcast.36), calls=%async_computation | async-start | bytes 2097152 | tf_op jit(solution)/shard_map/all_to_all | solution.py:31
  71.5 0.2 select_reduce_fusion.1
  71.9 42.0 %all-to-all-done = bf16[32,8,2048]{2,0,1:T(8,128)(2,1)S(1)} async-done(((bf16[32,8,2048]{2,0,1:T(8,128)(2,1)}), bf16[32,8,2048]{2,0,1:T(8,128)(2,1)S(1)}, u32[]{:S(2)}, u32[]{:S(2)}) %all-to-all-start) | async-done | bytes 1048608 | tf_op jit(solution)/shard_map/all_to_all | solution.py:31
  113.9 0.2 convert_element_type.65
  114.1 0.4 copy.47
  114.9 39.9 %all-gather.2.cloned.1.call-done = bf16[32,256,256]{2,1,0:T(8,128)(2,1)} async-done(((bf16[4,256,256]{2,1,0:T(8,128)(2,1)}), bf16[32,256,256]{2,1,0:T(8,128)(2,1)}) %all-gather.2.cloned.1.call-update) | async-done | bytes 4194320 | tf_op jit(solution)/shard_map/all_gather | solution.py:51
  154.8 5.8 %fusion.6 = bf16[16,256,256]{2,0,1:T(8,128)(2,1)S(1)} fusion(bf16[32,256,256]{2,1,0:T(8,128)(2,1)} %all-gather.2.cloned.1.call-done, f32[16,32]{1,0:T(8,128)S(1)} %select_reduce_fusion), kind=kOutput, calls=%fused_computation.9 | convolution fusion | flops 403701760 | bytes 6293504 | tf_op jit(solution)/shard_map/bo,okl->bkl/dot_general | solution.py:20
  160.5 1.7 multiply_bitcast_fusion
  162.2 2.5 %copy.41 = f32[256,16,128]{2,1,0:T(8,128)} copy(f32[256,16,128]{2,0,1:T(8,128)S(1)} %multiply_bitcast_fusion) | data formatting | bytes 4194304 | tf_op jit(solution)/shard_map/mul | solution.py:55
  164.8 1.7 mul.36
  166.5 0.3 fusion.3
  166.8 28.7 %all_to_all.58 = bf16[8,32,2048]{2,1,0:T(8,128)(2,1)S(1)} all-to-all(bf16[8,32,2048]{2,1,0:T(8,128)(2,1)S(1)} %fusion.3), channel_id=1, replica_groups=mesh['vox'=4,'mem'=8] {'mem'}, dimensions={0} | all-to-all | bytes 2097152 | tf_op jit(solution)/shard_map/all_to_all | solution.py:56
  195.4 1.0 copy.46
  (28 shorter events, 1.1 us)
Async XLA Ops:
  6.5 38.1 %copy-start.1 = (f32[32,4096]{1,0:T(8,128)S(1)}, f32[32,4096]{1,0:T(8,128)}, u32[]{:S(2)}) copy-start(f32[32,4096]{1,0:T(8,128)} %param.10) | copy-start | bytes 1572868
  6.5 38.1 %copy-start.3 = (f32[4096]{0:T(1024)S(1)}, f32[4096]{0:T(1024)}, u32[]{:S(2)}) copy-start(f32[4096]{0:T(1024)} %param.11) | copy-start | bytes 49156
  6.5 38.1 %copy-start.2 = (f32[4096]{0:T(1024)S(1)}, f32[4096]{0:T(1024)}, u32[]{:S(2)}) copy-start(f32[4096]{0:T(1024)} %param.12) | copy-start | bytes 49156
  6.5 30.9 %reduce-scatter.2.cloned.1.call-start = ((), (), s32[]{:S(2)}) async-start(), calls=%async_computation.5 | async-start | bytes 1310720 | tf_op jit(solution)/shard_map/reduce_scatter | solution.py:25
  39.1 14.3 %all-to-all-start.1 = ((bf16[32,8,512]{2,0,1:T(8,128)(2,1)}), bf16[32,8,512]{2,0,1:T(8,128)(2,1)S(1)}, u32[]{:S(2)}, u32[]{:S(2)}) async-start(bf16[32,8,512]{2,0,1:T(8,128)(2,1)} %bitcast.38), calls=%async_computation.2 | async-start | bytes 524288 | tf_op jit(solution)/shard_map/all_to_all | solution.py:46
  53.3 12.2 %all-to-all-start.2 = ((bf16[32,8,512]{2,0,1:T(8,128)(2,1)}), bf16[32,8,512]{2,0,1:T(8,128)(2,1)S(1)}, u32[]{:S(2)}, u32[]{:S(2)}) async-start(bf16[32,8,512]{2,0,1:T(8,128)(2,1)} %bitcast.37), calls=%async_computation.3 | async-start | bytes 524288 | tf_op jit(solution)/shard_map/all_to_all | solution.py:47
  56.9 97.8 %all-gather.2.cloned.1.call-start = ((), (), s32[]{:S(2)}) async-start(), calls=%async_computation.6 | async-start | bytes 4718592 | tf_op jit(solution)/shard_map/all_gather | solution.py:51
  57.0 9.8 %copy-start = (bf16[32,16384]{1,0:T(8,128)(2,1)S(1)}, bf16[32,16384]{1,0:T(8,128)(2,1)}, u32[]{:S(2)}) copy-start(bf16[32,16384]{1,0:T(8,128)(2,1)} %param.8) | copy-start | bytes 3145732
  66.8 4.7 %copy-start.5 = (s32[16,16]{1,0:T(8,128)S(1)}, s32[16,16]{1,0:T(8,128)}, u32[]{:S(2)}) copy-start(s32[16,16]{1,0:T(8,128)} %param.14) | copy-start | bytes 3076
  66.8 4.7 %copy-start.6 = (f32[16]{0:T(128)S(1)}, f32[16]{0:T(128)}, u32[]{:S(2)}) copy-start(f32[16]{0:T(128)} %param.15) | copy-start | bytes 196
  66.8 4.9 %copy-start.4 = (s32[16,16]{1,0:T(8,128)S(1)}, s32[16,16]{1,0:T(8,128)}, u32[]{:S(2)}) copy-start(s32[16,16]{1,0:T(8,128)} %param.13) | copy-start | bytes 3076
  67.9 46.0 %all-to-all-start = ((bf16[32,8,2048]{2,0,1:T(8,128)(2,1)}), bf16[32,8,2048]{2,0,1:T(8,128)(2,1)S(1)}, u32[]{:S(2)}, u32[]{:S(2)}) async-start(bf16[32,8,2048]{2,0,1:T(8,128)(2,1)} %bitcast.36), calls=%async_computation | async-start | bytes 2097152 | tf_op jit(solution)/shard_map/all_to_all | solution.py:31
Sparse Core Ops, SparseCore 0:
  9.9 27.4 reduce-scatter.1
  66.9 87.7 all-gather.1
where the time goes:
time: 204 us; the launch traced here: 203 us
  waiting for transfers between devices  125 us (61%)
  blocking collectives  28.7 us (14%)
  between operations  13.6 us (7%)
  starting transfers between devices  12.7 us (6%)
  local copies, waits for them, and re-layouts  9.4 us (5%)
  matrix products  8.55 us (4%)
  other arithmetic  5.17 us (3%)
    all_to_all x1, waiting for transfers between devices, local(): lax.all_to_all(ensemble, 'mem', split_axis=1, concat_axis=0, tiled=True)  42 us
    all_gather x1, waiting for transfers between devices, local(): lax.all_gather(own_moments.astype(jnp.bfloat16), 'mem', axis=0, tiled=True)  39.9 us
    all_to_all x1, blocking collectives, local(): lax.all_to_all(updated, 'mem', split_axis=0, concat_axis=1, tiled=True)  28.7 us
    reduce_scatter x1, waiting for transfers between devices, local(): lax.psum_scatter(partials[0].astype(jnp.bfloat16), 'vox', scatter_dimensi...  28.1 us
    all_to_all x1, waiting for transfers between devices, local(): lax.all_to_all(weights, 'mem', split_axis=1, concat_axis=0, tiled=True)  8.19 us
    all_to_all x1, waiting for transfers between devices, local(): lax.all_to_all(summed, 'mem', split_axis=1, concat_axis=0, tiled=True)  6.96 us
    dot_general x1, matrix products, from_moments(): jnp.einsum('bo,okl->bkl', coeff, moments, precision=high)  5.77 us
    all_to_all x1, starting transfers between devices, local(): lax.all_to_all(summed, 'mem', split_axis=1, concat_axis=0, tiled=True)  5.52 us
  transfers between devices with their start and end apart: 5, of which 5 were waited for; matrix products, arithmetic and copies ran while one was open for 2% of the time, Pallas kernels for 0%

commit v1 on v0

--- a/solution.py
+++ b/solution.py
@@ -2,6 +2,7 @@
 import jax.numpy as jnp
 from jax import lax
 from jax.sharding import PartitionSpec as P
+from jax.lax import all_to_all, axis_size
 
 OB = 128
 
@@ -42,8 +43,16 @@
         jnp.float32
     )
     coeff = jnp.sum(tapers[:, :, None] * picks, axis=1)
+
+    def read_pages(a_name, xs):
+        local_part = axis_size(a_name)
+        mat_out = jnp.split(xs, local_part, 1)
+        y2 = jnp.stack(mat_out, 0)
+        o_now = all_to_all(y2, a_name, 0, 0)
+        return jnp.concatenate(o_now, axis=0)
+
     pred_own, wts_own = (
-        lax.all_to_all(summed, "mem", split_axis=1, concat_axis=0, tiled=True),
+        read_pages("mem", xs=summed),
         lax.all_to_all(weights, "mem", split_axis=1, concat_axis=0, tiled=True),
     )
     own_anom = center(pred_own).reshape(count, -1, OB)

time: 204 us -> 214 us (1.049)
  local copies, waits for them, and re-layouts: 9.4 us -> 18.7 us
    unnamed x15 -> x22, local copies, waits for them, and re-layouts: 0.42 us -> 10 us
where the time goes in v1:
time: 214 us; the launch traced here: 213 us
  waiting for transfers between devices  125 us (58%)
  blocking collectives  28.7 us (13%)
  local copies, waits for them, and re-layouts  18.7 us (9%)
  between operations  13.6 us (6%)
  starting transfers between devices  12.7 us (6%)
  matrix products  8.56 us (4%)
  other arithmetic  5.03 us (2%)
    all_to_all x1, waiting for transfers between devices, local(): lax.all_to_all(ensemble, 'mem', split_axis=1, concat_axis=0, tiled=True)  42 us
    all_gather x1, waiting for transfers between devices, local(): lax.all_gather(own_moments.astype(jnp.bfloat16), 'mem', axis=0, tiled=True)  39.9 us
    all_to_all x1, blocking collectives, local(): lax.all_to_all(updated, 'mem', split_axis=0, concat_axis=1, tiled=True)  28.7 us
    reduce_scatter x1, waiting for transfers between devices, local(): lax.psum_scatter(partials[0].astype(jnp.bfloat16), 'vox', scatter_dimensi...  28.1 us
    unnamed x22, local copies, waits for them, and re-layouts  10 us
    all_to_all x1, waiting for transfers between devices, local(): lax.all_to_all(weights, 'mem', split_axis=1, concat_axis=0, tiled=True)  8.45 us
    all_to_all x1, waiting for transfers between devices, read_pages(): o_now = all_to_all(y2, a_name, 0, 0)  6.97 us
    dot_general x1, matrix products, from_moments(): jnp.einsum('bo,okl->bkl', coeff, moments, precision=high)  5.77 us
  transfers between devices with their start and end apart: 5, of which 5 were waited for; matrix products, arithmetic and copies ran while one was open for 2% of the time, Pallas kernels for 0%

profile of v1, /device:TPU:0, one launch (start us, length us, event | category | flops | bytes accessed | tf_op | source)
XLA Modules:
  0.0 212.7 jit_solution(7133624367926183861)
XLA Ops:
  6.5 2.7 %convert_bitcast_fusion = bf16[32,16384]{1,0:T(8,128)(2,1)} fusion(f32[1,32,16384]{2,1,0:T(8,128)} %param.9), kind=kLoop, calls=%fused_computation.13 | loop fusion | flops 524288 | bytes 3145728 | tf_op jit(solution)/shard_map/convert_element_type | solution.py:27
  9.3 28.1 %reduce-scatter.2.cloned.1.call-done = bf16[32,4096]{1,0:T(8,128)(2,1)} async-done(((bf16[32,16384]{1,0:T(8,128)(2,1)}), bf16[32,4096]{1,0:T(8,128)(2,1)}) %reduce-scatter.2.cloned.1.call-update) | async-done | bytes 262160 | tf_op jit(solution)/shard_map/reduce_scatter | solution.py:26
  37.4 1.4 fusion.23
  38.8 1.4 fusion.22
  40.1 1.4 fusion.21
  41.5 1.4 fusion.20
  42.9 1.4 fusion.19
  44.3 1.4 fusion.18
  45.6 1.4 fusion.17
  47.0 1.4 fusion.16
  48.4 5.5 %all-to-all-start.1 = ((bf16[8,32,512]{2,1,0:T(8,128)(2,1)}), bf16[8,32,512]{2,1,0:T(8,128)(2,1)S(1)}, u32[]{:S(2)}, u32[]{:S(2)}) async-start(bf16[8,32,512]{2,1,0:T(8,128)(2,1)} %fusion.16), calls=%async_computation.2 | async-start | bytes 524288 | tf_op jit(solution)/shard_map/all_to_all | solution.py:51
  55.7 7.0 %all-to-all-done.1 = bf16[8,32,512]{2,1,0:T(8,128)(2,1)S(1)} async-done(((bf16[8,32,512]{2,1,0:T(8,128)(2,1)}), bf16[8,32,512]{2,1,0:T(8,128)(2,1)S(1)}, u32[]{:S(2)}, u32[]{:S(2)}) %all-to-all-start.1) | async-done | bytes 262176 | tf_op jit(solution)/shard_map/all_to_all | solution.py:51
  62.7 3.6 %all-to-all-start.2 = ((bf16[32,8,512]{2,0,1:T(8,128)(2,1)}), bf16[32,8,512]{2,0,1:T(8,128)(2,1)S(1)}, u32[]{:S(2)}, u32[]{:S(2)}) async-start(bf16[32,8,512]{2,0,1:T(8,128)(2,1)} %bitcast.64), calls=%async_computation.3 | async-start | bytes 524288 | tf_op jit(solution)/shard_map/all_to_all | solution.py:56
  66.4 8.4 %all-to-all-done.2 = bf16[32,8,512]{2,0,1:T(8,128)(2,1)S(1)} async-done(((bf16[32,8,512]{2,0,1:T(8,128)(2,1)}), bf16[32,8,512]{2,0,1:T(8,128)(2,1)S(1)}, u32[]{:S(2)}, u32[]{:S(2)}) %all-to-all-start.2) | async-done | bytes 262176 | tf_op jit(solution)/shard_map/all_to_all | solution.py:56
  75.1 1.1 convolution_convert_fusion
  76.3 1.0 copy.61
  77.3 3.6 %all-to-all-start = ((bf16[32,8,2048]{2,0,1:T(8,128)(2,1)}), bf16[32,8,2048]{2,0,1:T(8,128)(2,1)S(1)}, u32[]{:S(2)}, u32[]{:S(2)}) async-start(bf16[32,8,2048]{2,0,1:T(8,128)(2,1)} %bitcast.63), calls=%async_computation | async-start | bytes 2097152 | tf_op jit(solution)/shard_map/all_to_all | solution.py:32
  81.3 42.0 %all-to-all-done = bf16[32,8,2048]{2,0,1:T(8,128)(2,1)S(1)} async-done(((bf16[32,8,2048]{2,0,1:T(8,128)(2,1)}), bf16[32,8,2048]{2,0,1:T(8,128)(2,1)S(1)}, u32[]{:S(2)}, u32[]{:S(2)}) %all-to-all-start) | async-done | bytes 1048608 | tf_op jit(solution)/shard_map/all_to_all | solution.py:32
  124.3 39.9 %all-gather.2.cloned.1.call-done = bf16[32,256,256]{2,1,0:T(8,128)(2,1)} async-done(((bf16[4,256,256]{2,1,0:T(8,128)(2,1)}), bf16[32,256,256]{2,1,0:T(8,128)(2,1)}) %all-gather.2.cloned.1.call-update) | async-done | bytes 4194320 | tf_op jit(solution)/shard_map/all_gather | solution.py:60
  164.2 5.8 %fusion.6 = bf16[16,256,256]{2,0,1:T(8,128)(2,1)S(1)} fusion(bf16[32,256,256]{2,1,0:T(8,128)(2,1)} %all-gather.2.cloned.1.call-done, f32[16,32]{1,0:T(8,128)S(1)} %select_reduce_fusion), kind=kOutput, calls=%fused_computation.9 | convolution fusion | flops 403701760 | bytes 6293504 | tf_op jit(solution)/shard_map/bo,okl->bkl/dot_general | solution.py:21
  169.9 1.7 multiply_bitcast_fusion
  171.6 2.5 %copy.37 = f32[256,16,128]{2,1,0:T(8,128)} copy(f32[256,16,128]{2,0,1:T(8,128)S(1)} %multiply_bitcast_fusion) | data formatting | bytes 4194304 | tf_op jit(solution)/shard_map/mul | solution.py:64
  174.2 1.7 mul.36
  176.2 28.7 %all_to_all.50 = bf16[8,32,2048]{2,1,0:T(8,128)(2,1)S(1)} all-to-all(bf16[8,32,2048]{2,1,0:T(8,128)(2,1)S(1)} %fusion.3), channel_id=1, replica_groups=mesh['vox'=4,'mem'=8] {'mem'}, dimensions={0} | all-to-all | bytes 2097152 | tf_op jit(solution)/shard_map/all_to_all | solution.py:65
  (33 shorter events, 4.8 us)
Async XLA Ops:
  6.5 47.4 %copy-start.1 = (f32[32,4096]{1,0:T(8,128)S(1)}, f32[32,4096]{1,0:T(8,128)}, u32[]{:S(2)}) copy-start(f32[32,4096]{1,0:T(8,128)} %param.10) | copy-start | bytes 1572868
  6.5 47.4 %copy-start.3 = (f32[4096]{0:T(1024)S(1)}, f32[4096]{0:T(1024)}, u32[]{:S(2)}) copy-start(f32[4096]{0:T(1024)} %param.11) | copy-start | bytes 49156
  6.5 47.4 %copy-start.2 = (f32[4096]{0:T(1024)S(1)}, f32[4096]{0:T(1024)}, u32[]{:S(2)}) copy-start(f32[4096]{0:T(1024)} %param.12) | copy-start | bytes 49156
  6.5 30.9 %reduce-scatter.2.cloned.1.call-start = ((), (), s32[]{:S(2)}) async-start(), calls=%async_computation.5 | async-start | bytes 1310720 | tf_op jit(solution)/shard_map/reduce_scatter | solution.py:26
  48.4 14.3 %all-to-all-start.1 = ((bf16[8,32,512]{2,1,0:T(8,128)(2,1)}), bf16[8,32,512]{2,1,0:T(8,128)(2,1)S(1)}, u32[]{:S(2)}, u32[]{:S(2)}) async-start(bf16[8,32,512]{2,1,0:T(8,128)(2,1)} %fusion.16), calls=%async_computation.2 | async-start | bytes 524288 | tf_op jit(solution)/shard_map/all_to_all | solution.py:51
  55.7 20.5 %copy-start = (bf16[32,16384]{1,0:T(8,128)(2,1)S(1)}, bf16[32,16384]{1,0:T(8,128)(2,1)}, u32[]{:S(2)}) copy-start(bf16[32,16384]{1,0:T(8,128)(2,1)} %param.8) | copy-start | bytes 3145732
  62.7 12.2 %all-to-all-start.2 = ((bf16[32,8,512]{2,0,1:T(8,128)(2,1)}), bf16[32,8,512]{2,0,1:T(8,128)(2,1)S(1)}, u32[]{:S(2)}, u32[]{:S(2)}) async-start(bf16[32,8,512]{2,0,1:T(8,128)(2,1)} %bitcast.64), calls=%async_computation.3 | async-start | bytes 524288 | tf_op jit(solution)/shard_map/all_to_all | solution.py:56
  66.3 97.9 %all-gather.2.cloned.1.call-start = ((), (), s32[]{:S(2)}) async-start(), calls=%async_computation.6 | async-start | bytes 4718592 | tf_op jit(solution)/shard_map/all_gather | solution.py:60
  76.2 4.7 %copy-start.5 = (s32[16,16]{1,0:T(8,128)S(1)}, s32[16,16]{1,0:T(8,128)}, u32[]{:S(2)}) copy-start(s32[16,16]{1,0:T(8,128)} %param.14) | copy-start | bytes 3076
  76.2 4.7 %copy-start.6 = (f32[16]{0:T(128)S(1)}, f32[16]{0:T(128)}, u32[]{:S(2)}) copy-start(f32[16]{0:T(128)} %param.15) | copy-start | bytes 196
  76.3 4.8 %copy-start.4 = (s32[16,16]{1,0:T(8,128)S(1)}, s32[16,16]{1,0:T(8,128)}, u32[]{:S(2)}) copy-start(s32[16,16]{1,0:T(8,128)} %param.13) | copy-start | bytes 3076
  77.3 46.0 %all-to-all-start = ((bf16[32,8,2048]{2,0,1:T(8,128)(2,1)}), bf16[32,8,2048]{2,0,1:T(8,128)(2,1)S(1)}, u32[]{:S(2)}, u32[]{:S(2)}) async-start(bf16[32,8,2048]{2,0,1:T(8,128)(2,1)} %bitcast.63), calls=%async_computation | async-start | bytes 2097152 | tf_op jit(solution)/shard_map/all_to_all | solution.py:32
Sparse Core Ops, SparseCore 0:
  9.9 27.4 reduce-scatter.1
  76.3 87.7 all-gather.1
